TPU v7x, 512 devices: a whole 4x8x8 slice. The times are simulated.
512 devices in a mesh: left: 16 (over x, y_hi, core), right: 32 (over y_lo, z).
Axes of the slice: x: 4, y: 8 (y_hi: 2, y_lo: 4; y = y_hi * 4 + y_lo), z: 8, core: 2. Of those that a mesh axis runs over, the one named last changes fastest.
Arguments:
- left_table: bfloat16 [32768, 256], P('left'), may hold values from -1.5 to 1.5
- right_table: bfloat16 [16, 16384, 256], P('left', 'right'), may hold values from -1.5 to 1.5
- relations: float32 [512, 256], replicated, may hold values from -6 to 6
- source_ids: int32 [16, 32, 1024], P('left', 'right'), may hold values from 0 to 2047
- relation_ids: int32 [16, 32, 1024], P('left', 'right'), may hold values from 0 to 511
- target_ids: int32 [16, 32, 1024], P('left', 'right'), may hold values from 0 to 511
- negative_ids: int32 [16, 32, 1, 1024], P('left', 'right'), may hold values from 0 to 511
- edge_counts: int32 [16, 32], P('left', 'right'), may hold values from 1 to 1024
Outputs:
- left_next: bfloat16 [32768, 256], P('left')
- right_next: bfloat16 [16, 16384, 256], P('left', 'right')
- relations_next: float32 [512, 256], replicated
Inputs may be any that keep to these rules, and one draw needn't show every extreme that they name: Edge slots at positions from edge_counts to 1023 hold ids but are padding.
All inputs are finite; a program needn't handle non-finite values.
Results may differ from a plain program's by a relative error of at most 0.0013.
Values may be sent and summed in bfloat16 or wider, within the bound.
No kernel may reach another device: no remote copies, remote signals or barrier semaphores. Data moves between devices by JAX's collectives and lax.ppermute only.
A program may use at most 64 MiB of HBM per device.

v0:
```python
import jax
import jax.numpy as jnp
from jax import lax
from jax.sharding import PartitionSpec as P

step_size = 0.5
relation_step = 12.0


def passed_along(array, axis, by):
    peers = lax.axis_size(axis)
    return lax.ppermute(array, axis, [(i, (i + by) % peers) for i in range(peers)])


def block_terms(left_blk, right_blk, relations, src, kind, dst, neg, live):
    half = relations.shape[1] // 2
    head = jnp.take(left_blk, src, axis=0).astype(jnp.float32)
    tail = jnp.take(right_blk, dst, axis=0).astype(jnp.float32)
    rel = jnp.take(relations, kind, axis=0)
    hre, him = (head[:, :half], head[:, half:])
    rre, rim = (rel[:, :half], rel[:, half:])
    query = jnp.concatenate([hre * rre - him * rim, hre * rim + him * rre], axis=1)
    q_low = query.astype(jnp.bfloat16)
    pos = jnp.sum(query * tail, axis=1)
    negrows = jnp.take(right_blk, neg, axis=0)
    scores = lax.dot_general(
        q_low, negrows, (((1,), (1,)), ((), ())), preferred_element_type=jnp.float32
    )
    c_pos = -jax.nn.sigmoid(-pos) * live
    c_neg = (jax.nn.sigmoid(scores) * (live[:, None] / neg.shape[0])).astype(jnp.bfloat16)
    g_query = jnp.dot(c_neg, negrows, preferred_element_type=jnp.float32) + c_pos[:, None] * tail
    g_neg = lax.dot_general(
        c_neg, q_low, (((0,), (0,)), ((), ())), preferred_element_type=jnp.float32
    )
    g_tail = c_pos[:, None] * query
    gre, gim = (g_query[:, :half], g_query[:, half:])
    grad_h = jnp.concatenate([gre * rre + gim * rim, -gre * rim + gim * rre], axis=1)
    grad_r = jnp.concatenate([gre * hre + gim * him, -gre * him + gim * hre], axis=1)
    return (grad_h, grad_r, g_tail, g_neg)


def shards(
    left_table,
    right_table,
    relations,
    source_ids,
    relation_ids,
    target_ids,
    negative_ids,
    edge_counts,
):
    right_blk = right_table[0]
    src_all = source_ids[0, 0]
    kind_all = relation_ids[0, 0]
    dst_all = target_ids[0, 0]
    negs = negative_ids[0, 0]
    count = edge_counts[0, 0]
    blocks = negs.shape[0]
    width = src_all.shape[0] // blocks
    live_blocks = (count + width - 1) // width

    def one(index, carry):
        lgrad, rgrad, tgrad = carry
        start = index * width
        n = lax.dynamic_index_in_dim(negs, index, 0, keepdims=False)
        live = (start + jnp.arange(width, dtype=jnp.int32) < count).astype(jnp.float32)
        grad_h, grad_r, g_tail, g_neg = block_terms(
            left_table, right_blk, relations, src_all, kind_all, dst_all, n, live
        )
        lgrad = lgrad.at[src_all].add(grad_h)
        rgrad = rgrad.at[kind_all].add(grad_r)
        tgrad = tgrad.at[dst_all].add(g_tail).at[n].add(g_neg)
        return (lgrad, rgrad, tgrad)

    init = (
        jnp.zeros(left_table.shape, jnp.float32),
        jnp.zeros(relations.shape, jnp.float32),
        jnp.zeros(right_blk.shape, jnp.float32),
    )
    left_grad, rel_grad, right_grad = lax.fori_loop(0, live_blocks, one, init)
    updated = (right_blk.astype(jnp.float32) - step_size * right_grad).astype(jnp.bfloat16)
    moved = passed_along(updated, "right", 1)
    left_total = lax.psum(left_grad, "right")
    rel_total = lax.psum(rel_grad, ("left", "right"))
    left_next = (left_table.astype(jnp.float32) - step_size * left_total).astype(jnp.bfloat16)
    relations_next = relations - relation_step * rel_total
    return (left_next, moved[None], relations_next)


def solution(mesh):
    return jax.shard_map(
        shards,
        mesh=mesh,
        in_specs=(
            P("left", None),
            P("left", "right", None),
            P(),
            P("left", "right", None),
            P("left", "right", None),
            P("left", "right", None),
            P("left", "right", None, None),
            P("left", "right"),
        ),
        out_specs=(P("left", None), P("left", "right", None), P()),
        check_vma=False,
    )
```

profile of v0, /device:TPU:2, one launch (start us, length us, event | category | flops | bytes accessed | tf_op | source)
XLA Modules:
  0.0 709.8 jit_solution(15141002125790694229)
XLA Ops:
  7.2 0.0 all-reduce.5.cloned.1.call-start
  7.9 0.7 compare_and_fusion.4
  8.6 0.7 fusion.13
  9.2 0.7 compare_select_fusion.9
  9.9 0.7 compare_and_fusion.6
  10.6 0.7 compare_select_fusion.8
  11.3 0.7 compare_and_fusion.5
  12.0 0.0 copy-start
  12.0 4.9 gather_fusion.4
  16.9 0.0 copy-start.1
  16.9 3.9 gather_fusion.6
  20.9 0.2 select_convert_fusion.1
  21.1 3.5 gather_fusion.5
  24.6 0.2 broadcast_select_fusion.4
  24.8 0.1 multiply_subtract_fusion.2
  24.9 0.0 copy-start.3
  24.9 0.0 copy-start.10
  24.9 0.0 copy-start.11
  25.0 0.0 copy-start.12
  25.0 0.0 copy-start.13
  25.0 0.4 fusion.12
  25.5 1.4 broadcast_in_dim.66
  26.9 80.2 %while.17 = (s32[]{:T(128)}, f32[2048,256]{1,0:T(8,128)}, f32[512,256]{1,0:T(8,128)S(1)}, f32[512,256]{1,0:T(8,128)S(1)}, s32[]{:T(128)}, /*index=5*/s32[1024]{0...) while((s32[]{:T(128)}, f32[2048,256]{1,0:T(8,128)}, ...), condition=%wide.region_6.8_spmd, body=%wide.region_1.7_spmd.sunk | while | flops 1624953856 | bytes 75646288 | solution.py:80
  27.3 0.7 negate_select_fusion.2
  28.0 5.0 gather_fusion
  32.9 3.9 gather_fusion.3
  36.9 1.0 copy.28
  37.9 5.0 gather_fusion.2
  42.9 1.2 copy.27
  44.1 1.0 select_convert_fusion.3
  45.2 4.7 gather_fusion.1
  49.8 2.6 copy.26
  52.4 1.4 broadcast_select_fusion.10
  53.8 0.1 copy-done.4
  54.0 0.2 multiply_subtract_fusion.4
  54.2 0.8 copy-done.5
  55.0 0.8 copy-done.6
  55.8 1.1 fusion.30
  56.9 2.5 copy.31
  59.4 6.7 scatter_fusion.2
  66.2 0.0 copy-start.9
  66.2 3.0 multiply_convert_fusion.2
  69.2 1.8 convolution_add_fusion.2
  71.0 1.8 fusion.31
  72.8 6.7 scatter_fusion.3
  79.5 3.0 multiply_add_fusion.7
  82.6 1.0 pad_maximum_fusion.5
  83.6 2.5 copy.29
  86.1 9.4 %scatter_fusion = f32[2048,256]{1,0:T(8,128)} fusion(f32[2048,256]{1,0:T(8,128)} %get-tuple-element.393, s32[1024]{0:T(1024)S(1)} %bitcast.59, f32[1024,256]{1,0:T(8,128)} %copy.29), kind=kCustom, calls=%fused_computation.7.clone.1 | custom fusion | flops 262144 | bytes 3149824 | tf_op jit(solution)/shard_map/while/body/scatter-add | solution.py:70
  95.5 2.1 pad_maximum_fusion.6
  97.6 2.5 copy.30
  100.1 6.7 scatter_fusion.1
  107.1 0.0 copy-start.2
  107.1 0.8 copy-done.2
  107.9 0.0 all-reduce.5.cloned.1.call-update
  107.9 0.0 all-reduce.3.cloned.1.call-start
  108.0 0.7 all-reduce.3.cloned.1.call-update
  108.7 0.1 subtract_convert_fusion.1
  108.8 4.3 collective-permute-start
  113.0 270.8 %all-reduce.5.cloned.1.call-done = f32[512,256]{1,0:T(8,128)} async-done(((f32[512,256]{1,0:T(8,128)}), f32[512,256]{1,0:T(8,128)}) %all-reduce.5.cloned.1.call-update) | async-done | bytes 524304 | tf_op jit(solution)/shard_map/psum | solution.py:84
  383.8 1.9 multiply_subtract_fusion.1
  385.7 313.7 %all-reduce.3.cloned.1.call-done = f32[2048,256]{1,0:T(8,128)} async-done(((f32[2048,256]{1,0:T(8,128)}), f32[2048,256]{1,0:T(8,128)}) %all-reduce.3.cloned.1.call-update) | async-done | bytes 2097168 | tf_op jit(solution)/shard_map/psum | solution.py:83
  699.4 2.8 subtract_convert_fusion
  702.2 0.7 copy.54
  (32 shorter events, 0.2 us)
Async XLA Ops:
  7.2 376.7 %all-reduce.5.cloned.1.call-start = ((), (), s32[]{:S(2)}) async-start(), calls=%async_computation.1 | async-start | bytes 1048576 | tf_op jit(solution)/shard_map/psum | solution.py:84
  12.0 4.9 copy-start
  16.9 4.2 copy-start.1
  24.9 2.0 copy-start.3
  24.9 2.0 copy-start.10
  24.9 2.0 copy-start.11
  25.0 2.0 copy-start.12
  25.0 2.0 copy-start.13
  52.4 1.5 copy-start.4
  54.0 1.0 copy-start.5
  55.0 0.8 copy-start.6
  66.2 3.0 copy-start.8
  66.2 3.0 copy-start.9
  69.2 1.8 copy-start.7
  107.1 0.8 copy-start.2
  107.9 591.5 %all-reduce.3.cloned.1.call-start = ((), (), s32[]{:S(2)}) async-start(), calls=%async_computation | async-start | bytes 4194304 | tf_op jit(solution)/shard_map/psum | solution.py:83
  108.8 277.0 %collective-permute-start = (bf16[512,256]{1,0:T(8,128)(2,1)S(1)}, bf16[512,256]{1,0:T(8,128)(2,1)S(1)}, u32[]{:S(2)}, u32[]{:S(2)}) collective-permute-start(bf16[512,256]{1,0:T(8,128)(2,1)S(1)} %subtract_convert_fusion.1), channel_id=1, source_target_pairs={{0,1},{1,2},{2,3},{3,4},{4,5},{5,6},{6,7},{7,8},{8,9},{9,10},{10,1... | collective-permute-start | bytes 786440 | tf_op jit(solution)/shard_map/ppermute | solution.py:12
Sparse Core Ops, SparseCore 0:
  108.1 275.7 all-reduce.4
  386.7 312.6 all-reduce.2
where the time goes:
time: 711 us; the launch traced here: 710 us
  waiting for transfers between devices  585 us (82%)
  other arithmetic  50.1 us (7%)
  local copies, waits for them, and re-layouts  48.1 us (7%)
  between operations  14.9 us (2%)
    psum x1, waiting for transfers between devices, shards(): left_total = lax.psum(left_grad, 'right')  314 us
    psum x1, waiting for transfers between devices, shards(): rel_total = lax.psum(rel_grad, ('left', 'right'))  271 us
  transfers between devices with their start and end apart: 3, of which 2 were waited for; matrix products, arithmetic and copies ran while one was open for 0% of the time, Pallas kernels for 0%

commit v1 on v0

--- a/solution.py
+++ b/solution.py
@@ -81,7 +81,7 @@
     updated = (right_blk.astype(jnp.float32) - step_size * right_grad).astype(jnp.bfloat16)
     moved = passed_along(updated, "right", 1)
     left_total = lax.psum(left_grad, "right")
-    rel_total = lax.psum(rel_grad, ("left", "right"))
+    rel_total = lax.psum(lax.psum(rel_grad, "right"), "left")
     left_next = (left_table.astype(jnp.float32) - step_size * left_total).astype(jnp.bfloat16)
     relations_next = relations - relation_step * rel_total
     return (left_next, moved[None], relations_next)

time: 711 us -> 623 us (0.88)
  the two profiles are of different devices: /device:TPU:2 before, /device:TPU:1 now
where the time goes in v1:
time: 623 us; the launch traced here: 622 us
  waiting for transfers between devices  497 us (80%)
  other arithmetic  50.1 us (8%)
  local copies, waits for them, and re-layouts  48.1 us (8%)
  between operations  14.9 us (2%)
  matrix products  6.52 us (1%)
    psum x1, waiting for transfers between devices, shards(): left_total = lax.psum(left_grad, 'right')  280 us
    psum x1, waiting for transfers between devices, shards(): rel_total = lax.psum(lax.psum(rel_grad, 'right'), 'left')  202 us
    ppermute x1, waiting for transfers between devices, passed_along(): lax.ppermute(array, axis, [(i, (i + by) % peers) for i in range(peers)])  15.7 us
    scatter-add x2, other arithmetic, one(): tgrad = tgrad.at[dst_all].add(g_tail).at[n].add(g_neg)  13.5 us
  transfers between devices with their start and end apart: 3, of which 3 were waited for; matrix products, arithmetic and copies ran while one was open for 0% of the time, Pallas kernels for 0%

profile of v1, /device:TPU:1, one launch (start us, length us, event | category | flops | bytes accessed | tf_op | source)
XLA Modules:
  0.0 622.0 jit_solution(6471389901041582001)
XLA Ops:
  7.2 0.0 all-reduce.6.cloned.1.call-start
  7.9 0.7 compare_and_fusion.4
  8.6 0.7 fusion.13
  9.2 0.7 compare_select_fusion.9
  9.9 0.7 compare_and_fusion.6
  10.6 0.7 compare_select_fusion.8
  11.3 0.7 compare_and_fusion.5
  12.0 0.0 copy-start
  12.0 4.9 gather_fusion.4
  16.9 0.0 copy-start.1
  16.9 3.9 gather_fusion.6
  20.9 0.2 select_convert_fusion.1
  21.1 3.5 gather_fusion.5
  24.6 0.2 broadcast_select_fusion.4
  24.8 0.1 multiply_subtract_fusion.2
  24.9 0.0 copy-start.3
  24.9 0.0 copy-start.10
  24.9 0.0 copy-start.11
  25.0 0.0 copy-start.12
  25.0 0.4 fusion.12
  25.5 1.4 broadcast_in_dim.66
  26.9 80.1 %while.17 = (s32[]{:T(128)}, f32[2048,256]{1,0:T(8,128)}, f32[512,256]{1,0:T(8,128)S(1)}, f32[512,256]{1,0:T(8,128)S(1)}, s32[]{:T(128)}, /*index=5*/s32[1024]{0...) while((s32[]{:T(128)}, f32[2048,256]{1,0:T(8,128)}, ...), condition=%wide.region_6.8_spmd, body=%wide.region_1.7_spmd.sunk | while | flops 1624953856 | bytes 75646288 | solution.py:80
  27.3 0.7 negate_select_fusion.2
  27.9 5.0 gather_fusion
  32.9 3.9 gather_fusion.3
  36.9 1.0 copy.28
  37.9 5.0 gather_fusion.2
  42.9 1.2 copy.27
  44.1 1.0 select_convert_fusion.3
  45.2 4.7 gather_fusion.1
  49.9 2.6 copy.26
  52.4 1.4 broadcast_select_fusion.10
  53.8 0.1 copy-done.4
  54.0 0.2 multiply_subtract_fusion.4
  54.2 0.8 copy-done.5
  55.0 0.8 copy-done.6
  55.8 1.1 fusion.30
  56.9 2.5 copy.31
  59.4 6.7 %scatter_fusion.2 = f32[512,256]{1,0:T(8,128)S(1)} fusion(f32[512,256]{1,0:T(8,128)S(1)} %get-tuple-element.397, s32[1024]{0:T(1024)S(1)} %bitcast.70, f32[1024,256]{1,0:T(8,128)} %copy.31), kind=kCustom, calls=%fused_computation.9.clone.1 | custom fusion | flops 262144 | bytes 3149824 | tf_op jit(solution)/shard_map/while/body/scatter-add | solution.py:72
  66.2 0.0 copy-start.9
  66.2 3.0 multiply_convert_fusion.2
  69.2 1.8 convolution_add_fusion.2
  71.0 1.7 fusion.31
  72.7 6.7 %scatter_fusion.3 = f32[512,256]{1,0:T(8,128)S(1)} fusion(f32[512,256]{1,0:T(8,128)S(1)} %scatter_fusion.2, s32[1024]{0:T(1024)S(1)} %bitcast.69, f32[1024,256]{1,0:T(8,128)} %fusion.31), kind=kCustom, calls=%fused_computation.10.clone.1 | custom fusion | flops 262144 | bytes 3149824 | tf_op jit(solution)/shard_map/while/body/scatter-add | solution.py:72
  79.5 3.0 multiply_add_fusion.7
  82.5 1.0 pad_maximum_fusion.5
  83.5 2.5 copy.29
  86.1 9.4 %scatter_fusion = f32[2048,256]{1,0:T(8,128)} fusion(f32[2048,256]{1,0:T(8,128)} %get-tuple-element.395, s32[1024]{0:T(1024)S(1)} %bitcast.59, f32[1024,256]{1,0:T(8,128)} %copy.29), kind=kCustom, calls=%fused_computation.7.clone.1 | custom fusion | flops 262144 | bytes 3149824 | tf_op jit(solution)/shard_map/while/body/scatter-add | solution.py:70
  95.4 2.1 pad_maximum_fusion.6
  97.5 2.5 copy.30
  100.1 6.7 %scatter_fusion.1 = f32[512,256]{1,0:T(8,128)S(1)} fusion(f32[512,256]{1,0:T(8,128)S(1)} %get-tuple-element.396, s32[1024]{0:T(1024)S(1)} %bitcast.57, f32[1024,256]{1,0:T(8,128)} %copy.30), kind=kCustom, calls=%fused_computation.8.clone.1 | custom fusion | flops 262144 | bytes 3149824 | tf_op jit(solution)/shard_map/while/body/scatter-add | solution.py:71
  107.1 0.0 copy-start.2
  107.1 0.8 copy-done.2
  107.8 0.0 all-reduce.6.cloned.1.call-update
  107.9 0.0 all-reduce.4.cloned.1.call-start
  107.9 0.1 subtract_convert_fusion.1
  108.0 4.8 collective-permute-start
  112.8 15.7 %collective-permute-done = bf16[512,256]{1,0:T(8,128)(2,1)S(1)} collective-permute-done((bf16[512,256]{1,0:T(8,128)(2,1)S(1)}, bf16[512,256]{1,0:T(8,128)(2,1)S(1)}, u32[]{:S(2)}, u32[]{:S(2)}) %collective-permute-start) | collective-permute-done | bytes 262176 | tf_op jit(solution)/shard_map/ppermute | solution.py:12
  128.5 279.6 %all-reduce.6.cloned.1.call-done = (f32[2048,256]{1,0:T(8,128)}, f32[512,256]{1,0:T(8,128)}) async-done(((f32[2048,256]{1,0:T(8,128)}, f32[512,256]{1,0:T(8,128)}), (f32[2048,256]{1,0:T(8,128)}, f32[512,256]{1,0:T(8,128)})) %all-reduce.6.cloned.1.call-update) | async-done | bytes 2621456 | tf_op jit(solution)/shard_map/psum | solution.py:83
  408.1 0.0 all-reduce.4.cloned.1.call-update
  408.1 2.8 subtract_convert_fusion
  410.9 201.6 %all-reduce.4.cloned.1.call-done = f32[512,256]{1,0:T(8,128)} async-done(((f32[512,256]{1,0:T(8,128)}), f32[512,256]{1,0:T(8,128)}) %all-reduce.4.cloned.1.call-update) | async-done | bytes 524304 | tf_op jit(solution)/shard_map/psum | solution.py:84
  612.5 1.9 multiply_subtract_fusion.1
  614.4 0.7 copy.55
  (32 shorter events, 0.2 us)
Async XLA Ops:
  7.2 400.9 %all-reduce.6.cloned.1.call-start = ((), (), s32[]{:S(2)}) async-start(), calls=%async_computation.1 | async-start | bytes 5242880 | tf_op jit(solution)/shard_map/psum | solution.py:83
  12.0 4.9 copy-start
  16.9 4.2 copy-start.1
  24.9 2.0 copy-start.3
  24.9 2.0 copy-start.10
  24.9 2.0 copy-start.11
  25.0 2.0 copy-start.12
  25.0 2.0 copy-start.13
  52.4 1.5 copy-start.4
  54.0 1.0 copy-start.5
  55.0 0.8 copy-start.6
  66.2 3.0 copy-start.8
  66.2 3.0 copy-start.9
  69.2 1.8 copy-start.7
  107.1 0.8 copy-start.2
  107.9 504.7 %all-reduce.4.cloned.1.call-start = ((), (), s32[]{:S(2)}) async-start(), calls=%async_computation | async-start | bytes 1048576 | tf_op jit(solution)/shard_map/psum | solution.py:84
  108.0 20.5 %collective-permute-start = (bf16[512,256]{1,0:T(8,128)(2,1)S(1)}, bf16[512,256]{1,0:T(8,128)(2,1)S(1)}, u32[]{:S(2)}, u32[]{:S(2)}) collective-permute-start(bf16[512,256]{1,0:T(8,128)(2,1)S(1)} %subtract_convert_fusion.1), channel_id=1, source_target_pairs={{0,1},{1,2},{2,3},{3,4},{4,5},{5,6},{6,7},{7,8},{8,9},{9,10},{10,1... | collective-permute-start | bytes 786440 | tf_op jit(solution)/shard_map/ppermute | solution.py:12
Sparse Core Ops, SparseCore 0:
  108.0 300.0 all-reduce.5
  411.0 201.5 all-reduce.3
